TPU v7x, 32 devices: a whole 2x2x4 slice. The times are simulated.
32 devices in a mesh: groups: 2 (over y), sub: 4 (over z), gauge: 2 (over x), tm: 2 (over core).
Axes of the slice: x: 2, y: 2, z: 4, core: 2. Of those that a mesh axis runs over, the one named last changes fastest.
Arguments:
- library: float32 [1024, 128, 256], P(('groups', 'sub'), 'gauge'), parts along dimension 0, may hold values from -0.25 to 0.25
- rates: float32 [16, 8, 512], P('groups', 'sub', 'tm'), parts along dimension 0, may hold values from -6 to 6
- subfault_ids: int32 [16, 8], P('groups', 'sub'), parts along dimension 0, may hold values from 0 to 511, as said below
- onsets: int32 [16, 8], P('groups', 'sub'), parts along dimension 0, may hold values from 0 to 511
Outputs:
- wave: float32 [128, 16, 512], P(('gauge', 'sub'), 'groups', 'tm'), parts along dimension 1
There are 2 independent parts, one for each index of `groups`. A program takes and returns all parts, laid end to end along the dimension named above; each array names one. Nothing has to cross between parts.
Inputs may be any that keep to these rules, and one draw needn't show every extreme that they name: `subfault_ids`: owner of an id is id // 128. In each aligned block of 2 columns, at most 12 of its 8 x 2 entries have one owner; one owner is named by exactly 12 entries of every block.
All inputs are finite; a program needn't handle non-finite values.
Results may differ from a plain program's by a relative error of at most 0.0003.
Values sent between devices are 32-bit elements; how exact they have to be, the bound alone decides.
A program may use at most 128 MiB of HBM per device.

v0:
```python
import jax
import jax.numpy as jnp
from jax import lax
from jax.sharding import PartitionSpec as P


def passed_along(block, axis, distance):
    devices = range(lax.axis_size(axis))
    route = [(i - distance, i) for i in devices if i - distance in devices]
    return lax.ppermute(block, axis, route)


def on_device(library, rates, subfault_ids, onsets):
    sub_count = lax.axis_size("sub")
    scen_count, entry_count, local_span = rates.shape
    sub_faults, panel_size, tap_count = library.shape
    capacity = 3 * scen_count * entry_count // sub_count
    entry_total = scen_count * entry_count
    slot_total = sub_count * capacity
    record_width = local_span + tap_count
    sample_times = lax.axis_index("tm") * local_span + lax.iota(jnp.int32, local_span)
    masked = jnp.where(
        sample_times[None, None, :] >= onsets[:, :, None], rates, jnp.zeros_like(rates)
    )
    tail_rows = masked[:, :, local_span - (tap_count - 1) :]
    prior_rows = passed_along(tail_rows, "tm", 1)
    closing = jnp.zeros((scen_count, entry_count, 1), jnp.float32)
    extended = jnp.concatenate([prior_rows, masked, closing], axis=2).reshape(
        entry_total, record_width
    )
    flat_ids = subfault_ids.reshape(entry_total)
    owner_of = flat_ids // sub_faults
    local_index = flat_ids % sub_faults
    owner_hits = (owner_of[:, None] == lax.iota(jnp.int32, sub_count)[None, :]).astype(jnp.int32)
    running = jnp.cumsum(owner_hits, axis=0)
    slot_rank = jnp.sum(running * owner_hits, axis=1) - 1
    slot_index = owner_of * capacity + slot_rank
    scenario_of = lax.iota(jnp.int32, entry_total) // entry_count
    scenario_axis = lax.iota(jnp.int32, scen_count)
    codes = (scenario_of * sub_faults + local_index + 1).astype(jnp.float32)
    send_records = jnp.zeros((slot_total, record_width), jnp.float32).at[slot_index].set(extended)
    send_codes = jnp.zeros((slot_total,), jnp.float32).at[slot_index].set(codes)
    records, got_codes = (
        lax.all_to_all(send_records, "sub", split_axis=0, concat_axis=0, tiled=True),
        lax.all_to_all(send_codes, "sub", split_axis=0, concat_axis=0, tiled=True),
    )
    code_value = got_codes.astype(jnp.int32) - 1
    filled = code_value >= 0
    safe_code = jnp.maximum(code_value, 0)
    kernels = library[safe_code % sub_faults]
    weights = (
        ((safe_code // sub_faults)[None, :] == scenario_axis[:, None]) & filled[None, :]
    ).astype(jnp.float32)
    slot_number = records.shape[0]
    block_count = local_span // tap_count
    sample_blocks = records.reshape(slot_number, block_count + 1, tap_count)
    paired = jnp.concatenate([sample_blocks[:, 0], sample_blocks[:, 1]], axis=1)
    tiled = jnp.tile(paired, (1, tap_count))[:, : tap_count * (2 * tap_count - 1)]
    window = tiled.reshape(slot_number, tap_count, 2 * tap_count - 1)[:, :, tap_count - 1 :]
    waves = jnp.einsum("sgk,skr->sgr", kernels, window, precision=lax.Precision.HIGHEST)
    pieces = jnp.einsum("cs,sgr->gcr", weights, waves, precision=lax.Precision.HIGHEST)
    return lax.psum_scatter(pieces, "sub", scatter_dimension=0, tiled=True)


def solution(mesh):
    in_specs = (
        P(("groups", "sub"), "gauge", None),
        P("groups", "sub", "tm"),
        P("groups", "sub"),
        P("groups", "sub"),
    )
    out_specs = P(("gauge", "sub"), "groups", "tm")
    return jax.shard_map(
        on_device, mesh=mesh, in_specs=in_specs, out_specs=out_specs, check_vma=False
    )
```

profile of v0, /device:TPU:0, one launch (start us, length us, event | category | flops | bytes accessed | tf_op | source)
XLA Modules:
  0.0 150.6 jit_solution(11623513256165155859)
XLA Ops:
  6.5 0.8 copy.19
  7.3 0.1 reshape.213
  7.4 0.1 reshape.212
  7.5 0.1 fusion.9
  7.6 0.2 select_reduce_fusion
  7.8 0.6 scatter_custom_fusion
  8.4 0.7 all_to_all.12
  9.1 6.3 %all-to-all-start = ((f32[4,12,1]{1,2,0:T(1,128)}), f32[4,12,1]{1,2,0:T(1,128)S(1)}, u32[]{:S(2)}, u32[]{:S(2)}) async-start(f32[4,12,1]{1,2,0:T(1,128)} %bitcast.2), calls=%async_computation | async-start | bytes 4096 | tf_op jit(solution)/shard_map/all_to_all | solution.py:45
  15.4 0.8 copy.22
  16.2 0.8 compare_select_fusion
  17.0 0.1 slice.22
  17.0 1.5 collective-permute-start
  18.5 0.1 pad.4.clone
  18.6 2.3 %all-to-all-done = f32[4,12,1]{1,2,0:T(1,128)S(1)} async-done(((f32[4,12,1]{1,2,0:T(1,128)}), f32[4,12,1]{1,2,0:T(1,128)S(1)}, u32[]{:S(2)}, u32[]{:S(2)}) %all-to-all-start) | async-done | bytes 224 | tf_op jit(solution)/shard_map/all_to_all | solution.py:45
  20.9 0.1 rem.79
  21.1 0.1 div.45
  21.2 0.1 reshape.221
  21.3 0.1 ge.27
  21.3 4.1 %gather_fusion = f32[48,64,256]{2,1,0:T(8,128)S(1)} fusion(f32[128,64,256]{2,1,0:T(8,128)} %param.4, s32[1024]{0:T(1024)S(1)} %pad_clamp_fusion), kind=kCustom, calls=%fused_computation | custom fusion | bytes 6291648 | tf_op jit(solution)/shard_map/gather | solution.py:50
  25.5 0.0 collective-permute-done
  25.5 0.1 maximum_maximum_fusion
  25.6 0.7 scatter_custom_fusion.1
  26.3 0.7 all_to_all.14
  27.0 3.3 %all-to-all-start.1 = ((f32[4,12,512]{2,1,0:T(8,128)}), f32[4,12,512]{2,1,0:T(8,128)S(1)}, u32[]{:S(2)}, u32[]{:S(2)}) async-start(f32[4,12,512]{2,1,0:T(8,128)} %all_to_all.14), calls=%async_computation.1 | async-start | bytes 262144 | tf_op jit(solution)/shard_map/all_to_all | solution.py:44
  30.3 0.0 reduce-scatter.2.cloned.1.call-start
  30.4 5.8 %all-to-all-done.1 = f32[4,12,512]{2,1,0:T(8,128)S(1)} async-done(((f32[4,12,512]{2,1,0:T(8,128)}), f32[4,12,512]{2,1,0:T(8,128)S(1)}, u32[]{:S(2)}, u32[]{:S(2)}) %all-to-all-start.1) | async-done | bytes 98336 | tf_op jit(solution)/shard_map/all_to_all | solution.py:44
  36.2 0.1 reshape.215
  36.3 0.1 fusion.24
  36.4 11.5 %tile.4 = f32[48,256,512]{2,1,0:T(8,128)} broadcast(f32[48,512]{1,0:T(8,128)S(1)} %pad_maximum_fusion), dimensions={0,2} | broadcast | bytes 25264128 | tf_op jit(solution)/shard_map/tile | solution.py:58
  47.9 21.7 %copy.27 = f32[6,8,256,512]{3,1,2,0:T(8,128)S(1)} copy(f32[6,8,256,512]{3,2,1,0:T(8,128)} %bitcast.22) | data formatting | bytes 50331648
  69.6 8.5 %slice.25 = f32[48,130816]{1,0:T(8,128)} slice(f32[48,131072]{1,0:T(8,128)S(1)} %bitcast.23), slice={[0:48], [0:130816]} | slice | bytes 50233344 | tf_op jit(solution)/shard_map/slice | solution.py:58
  78.1 27.0 %reshape.216 = f32[48,256,511]{2,1,0:T(8,128)} reshape(f32[48,130816]{1,0:T(8,128)} %slice.25) | data formatting | bytes 50233344 | tf_op jit(solution)/shard_map/reshape | solution.py:59
  105.1 13.9 %fusion = f32[48,64,256]{2,1,0:T(8,128)S(1)} fusion(f32[48,64,256]{2,1,0:T(8,128)S(1)} %gather_fusion, f32[48,256,511]{2,1,0:T(8,128)} %reshape.216), kind=kOutput, calls=%fused_computation.3 | convolution fusion | flops 2415919104 | bytes 18874368 | tf_op jit(solution)/shard_map/sgk,skr->sgr/dot_general | solution.py:60
  119.0 3.7 %fusion.4 = f32[64,8,256]{2,1,0:T(8,128)} fusion(f32[48,64,256]{2,1,0:T(8,128)S(1)} %fusion, s32[48]{0:T(128)S(1)} %add_select_fusion, pred[48]{0:T(512)(128)(4,1)S(1)} %ge.27), kind=kOutput, calls=%fused_computation.7 | convolution fusion | flops 75498240 | bytes 3670256 | tf_op jit(solution)/shard_map/cs,sgr->gcr/dot_general | solution.py:61
  122.7 0.0 reduce-scatter.2.cloned.1.call-update
  122.7 21.1 %reduce-scatter.2.cloned.1.call-done = f32[16,8,256]{2,1,0:T(8,128)} async-done(((f32[64,8,256]{2,1,0:T(8,128)}), f32[16,8,256]{2,1,0:T(8,128)}) %reduce-scatter.2.cloned.1.call-update) | async-done | bytes 131088 | tf_op jit(solution)/shard_map/reduce_scatter | solution.py:62
  (12 shorter events, 0.2 us)
Async XLA Ops:
  9.1 11.8 %all-to-all-start = ((f32[4,12,1]{1,2,0:T(1,128)}), f32[4,12,1]{1,2,0:T(1,128)S(1)}, u32[]{:S(2)}, u32[]{:S(2)}) async-start(f32[4,12,1]{1,2,0:T(1,128)} %bitcast.2), calls=%async_computation | async-start | bytes 4096 | tf_op jit(solution)/shard_map/all_to_all | solution.py:45
  17.0 8.4 %collective-permute-start = (f32[8,2,255]{2,1,0:T(2,128)S(1)}, f32[8,2,255]{2,1,0:T(2,128)S(1)}, u32[]{:S(2)}, u32[]{:S(2)}) collective-permute-start(f32[8,2,255]{2,1,0:T(2,128)S(1)} %slice.22), channel_id=1, source_target_pairs={{0,1},{2,3},{4,5},{6,7},{8,9},{10,11},{12,13},{14,15},{16,17},{18,... | collective-permute-start | bytes 48968 | tf_op jit(solution)/shard_map/ppermute | solution.py:10
  27.0 9.2 %all-to-all-start.1 = ((f32[4,12,512]{2,1,0:T(8,128)}), f32[4,12,512]{2,1,0:T(8,128)S(1)}, u32[]{:S(2)}, u32[]{:S(2)}) async-start(f32[4,12,512]{2,1,0:T(8,128)} %all_to_all.14), calls=%async_computation.1 | async-start | bytes 262144 | tf_op jit(solution)/shard_map/all_to_all | solution.py:44
  30.3 113.4 %reduce-scatter.2.cloned.1.call-start = ((), (), s32[]{:S(2)}) async-start(), calls=%async_computation.3 | async-start | bytes 655360 | tf_op jit(solution)/shard_map/reduce_scatter | solution.py:62
Sparse Core Ops, SparseCore 0:
  122.8 20.8 reduce-scatter.1
where the time goes:
time: 151 us
  local copies, waits for them, and re-layouts  77.8 us (52%)
  waiting for transfers between devices  29.2 us (19%)
  matrix products  17.6 us (12%)
  between operations  13.5 us (9%)
  starting transfers between devices  11.2 us (7%)
    reshape x1, local copies, waits for them, and re-layouts, on_device(): tiled.reshape(slot_number, tap_count, 2 * tap_count - 1)  27 us
    unnamed x3, local copies, waits for them, and re-layouts  23.2 us
    reduce_scatter x1, waiting for transfers between devices, on_device(): return lax.psum_scatter(pieces, 'sub', scatter_dimension=0, tiled=True)  21.1 us
    dot_general x1, matrix products, on_device(): jnp.einsum('sgk,skr->sgr', kernels, window, precision=lax.Precision.HIGHEST)  13.9 us
    another operation x1, local copies, waits for them, and re-layouts, on_device(): jnp.tile(paired, (1, tap_count))[:, :tap_count * (2 * tap_count - 1)]  11.5 us
    slice x1, local copies, waits for them, and re-layouts, on_device(): jnp.tile(paired, (1, tap_count))[:, :tap_count * (2 * tap_count - 1)]  8.48 us
    all_to_all x1, starting transfers between devices, on_device(): lax.all_to_all(send_codes, 'sub', split_axis=0, concat_axis=0, tiled=True)  6.35 us
    all_to_all x1, waiting for transfers between devices, on_device(): lax.all_to_all(send_records, 'sub', split_axis=0, concat_axis=0, tiled=True)  5.82 us
  transfers between devices with their start and end apart: 4, of which 3 were waited for; matrix products, arithmetic and copies ran while one was open for 4% of the time, Pallas kernels for 0%

commit v1 on v0

v1 whole, which is shorter than its diff:
```python
import functools

import jax
import jax.numpy as jnp
from jax import lax
from jax.experimental import pallas as pl
from jax.experimental.pallas import tpu as pltpu
from jax.sharding import PartitionSpec as P

MESH = pl.DeviceIdType.MESH


def synth_kernel(
    sub_n, tm_n, lib_hbm, rates, ids, onsets, out,
    lib, cur, prior, ids_s, ons_s, toe_hi, toe_lo, green, part, recv,
    lib_sem, own_sem, cur_send, cur_recv, prior_send, prior_recv, wave_send, wave_recv,
):
    me = lax.axis_index("sub")
    core = lax.axis_index("tm")
    scen_n, edev, span = rates.shape
    faults, panel, taps = lib.shape
    rows = panel // sub_n
    half = taps // 2

    lib_copy = pltpu.make_async_copy(lib_hbm, lib, lib_sem)
    lib_copy.start()
    own = [
        pltpu.make_async_copy(rates, cur.at[me], own_sem.at[0]),
        pltpu.make_async_copy(ids, ids_s.at[me], own_sem.at[1]),
        pltpu.make_async_copy(onsets, ons_s.at[me], own_sem.at[2]),
    ]
    for c in own:
        c.start()
    prior[...] = jnp.zeros_like(prior)

    barrier = pltpu.get_barrier_semaphore()

    def peer(o):
        return lax.rem(me + o, sub_n)

    for o in range(1, sub_n):
        pl.semaphore_signal(barrier, inc=1, device_id={"sub": peer(o)}, device_id_type=MESH)
    for step in (-1, 1):
        @pl.when((core + step >= 0) & (core + step < tm_n))
        def _():
            for o in range(sub_n):
                pl.semaphore_signal(
                    barrier, inc=1, device_id={"sub": peer(o), "tm": core + step}, device_id_type=MESH
                )
    ends = jnp.where(core > 0, sub_n, 0) + jnp.where(core < tm_n - 1, sub_n, 0)
    pl.semaphore_wait(barrier, sub_n - 1 + ends)

    def same_tm(o):
        who = {"sub": peer(o)}
        return [
            pltpu.make_async_remote_copy(
                src_ref=src, dst_ref=dst.at[me], send_sem=cur_send.at[i, o - 1],
                recv_sem=cur_recv.at[i, o - 1], device_id=who, device_id_type=MESH,
            )
            for i, (src, dst) in enumerate(((ids, ids_s), (onsets, ons_s), (rates, cur)))
        ]

    def next_tm(o):
        return pltpu.make_async_remote_copy(
            src_ref=rates, dst_ref=prior.at[me], send_sem=prior_send.at[o],
            recv_sem=prior_recv.at[o], device_id={"sub": peer(o), "tm": core + 1}, device_id_type=MESH,
        )

    def from_tm(o):
        return pltpu.make_async_remote_copy(
            src_ref=rates, dst_ref=prior.at[lax.rem(me - o + sub_n, sub_n)], send_sem=prior_send.at[o],
            recv_sem=prior_recv.at[o], device_id={"sub": peer(o), "tm": core}, device_id_type=MESH,
        )

    def from_same(o):
        src_dev = lax.rem(me - o + sub_n, sub_n)
        return [
            pltpu.make_async_remote_copy(
                src_ref=src, dst_ref=dst.at[src_dev], send_sem=cur_send.at[i, o - 1],
                recv_sem=cur_recv.at[i, o - 1], device_id={"sub": peer(o)}, device_id_type=MESH,
            )
            for i, (src, dst) in enumerate(((ids, ids_s), (onsets, ons_s), (rates, cur)))
        ]

    for o in range(sub_n - 1, 0, -1):
        for c in same_tm(o):
            c.start()

    @pl.when(core < tm_n - 1)
    def _():
        for o in range(sub_n - 1, -1, -1):
            next_tm(o).start()

    for c in own:
        c.wait()
    for o in range(1, sub_n):
        for c in from_same(o):
            c.wait_recv()

    @pl.when(core > 0)
    def _():
        for o in range(sub_n):
            from_tm(o).wait_recv()

    lib_copy.wait()

    times = lax.broadcasted_iota(jnp.int32, (1, 2 * span), 1) + (core - 1) * span

    def toeplitz(z, s, e, slot):
        name = ids_s[z, s, e]
        mine = (name // faults) == me
        first = jnp.where(mine, ons_s[z, s, e], jnp.int32(2**30))
        record = jnp.concatenate(
            [prior[z, s, pl.ds(e, 1), :], cur[z, s, pl.ds(e, 1), :]], axis=1
        )
        record = jnp.where(times >= first, record, 0.0)
        skewed = pltpu.roll(
            jnp.broadcast_to(record, (8, 2 * span)), 0, 1, stride=1, stride_axis=0
        )
        for pair in range(half // 16):
            two = [
                (pltpu.roll(skewed, 16 * pair + 8 * h, 1) if pair + h else skewed)[:, half:]
                for h in range(2)
            ]
            both = jnp.concatenate(two, axis=0)
            high = both.astype(jnp.bfloat16)
            toe_hi[slot, pl.ds(16 * pair, 16), :] = high
            toe_lo[slot, pl.ds(16 * pair, 16), :] = (both - high.astype(jnp.float32)).astype(jnp.bfloat16)
        where = jnp.clip(name - me * faults, 0, faults - 1)
        function = lib[where]
        high = function.astype(jnp.bfloat16)
        green[pl.ds(0, panel), pl.ds(slot * taps, taps)] = high
        green[pl.ds(panel, panel), pl.ds(slot * taps, taps)] = (
            function - high.astype(jnp.float32)
        ).astype(jnp.bfloat16)

    group = max(u for u in range(1, 5) if sub_n % u == 0)
    slots = group * edev

    def stacked(toe):
        pieces = []
        for slot in range(slots):
            pieces.append(toe[slot, :, pl.ds(half, span)])
            pieces.append(toe[slot, :, pl.ds(0, span)])
        return jnp.concatenate(pieces, axis=0)

    def wave_copy(s, o, dest, sent):
        return pltpu.make_async_remote_copy(
            src_ref=part.at[s, dest],
            dst_ref=recv.at[o - 1, s], send_sem=wave_send.at[o - 1], recv_sem=wave_recv.at[o - 1],
            device_id={"sub": dest}, device_id_type=MESH,
        )

    def scenario(s, carry):
        def block_group(first_z):
            for i in range(group):
                for e in range(edev):
                    toeplitz(first_z + i, s, e, i * edev + e)
            big = jnp.dot(green[...], stacked(toe_hi), preferred_element_type=jnp.float32)
            small = jnp.dot(green[pl.ds(0, panel), :], stacked(toe_lo), preferred_element_type=jnp.float32)
            return big[:panel] + (big[panel:] + small)

        def panels(wave):
            return [wave[rows * d : rows * (d + 1)] for d in range(sub_n)]

        for d, piece in enumerate(panels(block_group(0))):
            part[s, d] = piece
        if sub_n > group:
            def more(i, c):
                for d, piece in enumerate(panels(block_group(i * group))):
                    part[s, d] += piece
                return c
            lax.fori_loop(1, sub_n // group, more, 0)
        for o in range(sub_n - 1, 0, -1):
            wave_copy(s, o, peer(o), True).start()
        return carry

    lax.fori_loop(0, scen_n, scenario, 0)

    def whole_wave(o):
        return pltpu.make_async_remote_copy(
            src_ref=recv.at[o - 1], dst_ref=recv.at[o - 1], send_sem=wave_send.at[o - 1],
            recv_sem=wave_recv.at[o - 1], device_id={"sub": peer(o)}, device_id_type=MESH,
        )

    total = part[:, me]
    for o in range(1, sub_n):
        whole_wave(o).wait_recv()
    for o in range(1, sub_n):
        total = total + recv[o - 1]
    out[...] = total
    for o in range(1, sub_n):
        whole_wave(o).wait_send()
        for c in same_tm(o):
            c.wait_send()

    @pl.when(core < tm_n - 1)
    def _():
        for o in range(sub_n):
            next_tm(o).wait_send()


def solution(mesh):
    sub_n, tm_n = mesh.shape["sub"], mesh.shape["tm"]

    def on_device(library, rates, subfault_ids, onsets):
        faults, panel, taps = library.shape
        scen_n, edev, span = rates.shape
        rows = panel // sub_n
        group = max(u for u in range(1, 5) if sub_n % u == 0)
        slots = group * edev
        dma = pltpu.SemaphoreType.DMA
        waves = pl.pallas_call(
            functools.partial(synth_kernel, sub_n, tm_n),
            out_shape=jax.ShapeDtypeStruct((scen_n, rows, span), jnp.float32),
            in_specs=[pl.BlockSpec(memory_space=pl.ANY)] * 4,
            out_specs=pl.BlockSpec(memory_space=pltpu.VMEM),
            scratch_shapes=[
                pltpu.VMEM((faults, panel, taps), jnp.float32),
                pltpu.VMEM((sub_n, scen_n, edev, span), jnp.float32),
                pltpu.VMEM((sub_n, scen_n, edev, span), jnp.float32),
                pltpu.SMEM((sub_n, scen_n, edev), jnp.int32),
                pltpu.SMEM((sub_n, scen_n, edev), jnp.int32),
                pltpu.VMEM((slots, taps // 2, span + taps // 2), jnp.bfloat16),
                pltpu.VMEM((slots, taps // 2, span + taps // 2), jnp.bfloat16),
                pltpu.VMEM((2 * panel, slots * taps), jnp.bfloat16),
                pltpu.VMEM((scen_n, sub_n, rows, span), jnp.float32),
                pltpu.VMEM((sub_n - 1, scen_n, rows, span), jnp.float32),
                dma, dma((3,)), dma((3, sub_n - 1)), dma((3, sub_n - 1)),
                dma((sub_n,)), dma((sub_n,)), dma((sub_n - 1,)), dma((sub_n - 1,)),
            ],
            compiler_params=pltpu.CompilerParams(collective_id=0, has_side_effects=True),
        )(library, rates, subfault_ids, onsets)
        return jnp.transpose(waves, (1, 0, 2))

    in_specs = (
        P(("groups", "sub"), "gauge", None),
        P("groups", "sub", "tm"),
        P("groups", "sub"),
        P("groups", "sub"),
    )
    out_specs = P(("gauge", "sub"), "groups", "tm")
    return jax.shard_map(
        on_device, mesh=mesh, in_specs=in_specs, out_specs=out_specs, check_vma=False
    )
```

time: 151 us -> 30 us (0.20)
  local copies, waits for them, and re-layouts: 77.8 us -> 4.32 us
  waiting for transfers between devices: 29.2 us -> 0 us
  Pallas kernels: 0 us -> 25.5 us
  matrix products: 17.6 us -> 0 us
  between operations: 13.5 us -> 0.01 us
  starting transfers between devices: 11.2 us -> 0 us
    reshape x5 -> x0, local copies, waits for them, and re-layouts: 27.2 us -> none  [the longest x1 27 us: on_device(): tiled.reshape(slot_number, tap_count, 2 * tap_count - 1)]
    pallas_call x0 -> x1, Pallas kernels: none -> 25.5 us  [on_device(): pl.pallas_call(functools.partial(synth_kernel, sub_n, tm_n), out_shape=ja...]
    reduce_scatter x1 -> x0, waiting for transfers between devices: 21.1 us -> none  [on_device(): return lax.psum_scatter(pieces, 'sub', scatter_dimension=0, tiled=True)]
    unnamed x3 -> x2, local copies, waits for them, and re-layouts: 23.2 us -> 2.68 us
    dot_general x2 -> x0, matrix products: 17.6 us -> none  [the longest x1 13.9 us: on_device(): jnp.einsum('sgk,skr->sgr', kernels, window, precision=lax.Precision.HIGHEST)]
    another operation x1 -> x0, local copies, waits for them, and re-layouts: 11.5 us -> none  [on_device(): jnp.tile(paired, (1, tap_count))[:, :tap_count * (2 * tap_count - 1)]]
    all_to_all x2 -> x0, starting transfers between devices: 9.67 us -> none  [the longest x1 6.35 us: on_device(): lax.all_to_all(send_codes, 'sub', split_axis=0, concat_axis=0, tiled=True)]
    slice x3 -> x0, local copies, waits for them, and re-layouts: 8.63 us -> none  [the longest x1 8.48 us: on_device(): jnp.tile(paired, (1, tap_count))[:, :tap_count * (2 * tap_count - 1)]]
  transfers between devices with their start and end apart: 4 -> 0, of which waited for: 3 -> 0; matrix products, arithmetic and copies ran while one was open for 4% -> 0% of each run, Pallas kernels for 0% -> 0%
where the time goes in v1:
time: 30 us; the launch traced here: 29.9 us
  Pallas kernels  25.5 us (85%)
  local copies, waits for them, and re-layouts  4.32 us (14%)
    pallas_call x1, Pallas kernels, on_device(): pl.pallas_call(functools.partial(synth_kernel, sub_n, tm_n), out_shape=ja...  25.5 us
    unnamed x2, local copies, waits for them, and re-layouts  2.68 us
    transpose x1, local copies, waits for them, and re-layouts, on_device(): return jnp.transpose(waves, (1, 0, 2))  1.64 us

profile of v1, /device:TPU:0, one launch (start us, length us, event | category | flops | bytes accessed | tf_op | source)
XLA Modules:
  0.0 29.9 jit_solution(13328225492402467323)
XLA Ops:
  0.0 1.3 %copy.5.ids = s32[8,2]{1,0:T(8,128)} copy(s32[8,2]{0,1:T(2,128)} %param.6) | data formatting | bytes 128 | tf_op args[2]
  1.3 1.3 %copy.6.onsets = s32[8,2]{1,0:T(8,128)} copy(s32[8,2]{0,1:T(2,128)} %param.7) | data formatting | bytes 128 | tf_op args[3]
  2.7 25.5 %shard_map.46 = f32[8,16,256]{2,1,0:T(8,128)} custom-call(f32[128,64,256]{2,1,0:T(8,128)} %lib_hbm.1, f32[8,2,256]{2,1,0:T(2,128)} %rates.1, s32[8,2]{1,0:T(8,128)} %copy.5.ids, s32[8,2]{1,0:T(8,128)} %copy.6.onsets), custom_call_target="tpu_custom_call" | custom-call | tf_op jit(solution)/shard_map/pallas_call | solution.py:213
  28.2 1.6 %copy.7 = f32[16,8,256]{2,1,0:T(8,128)} copy(f32[16,8,256]{2,0,1:T(8,128)} %bitcast.1) | data formatting | bytes 262144 | tf_op jit(solution)/shard_map/transpose | solution.py:234

commit v2 on v1

--- a/solution.py
+++ b/solution.py
@@ -107,9 +107,9 @@
     times = lax.broadcasted_iota(jnp.int32, (1, 2 * span), 1) + (core - 1) * span
 
     def toeplitz(z, s, e, slot):
-        name = ids_s[z, s, e]
+        name = ids_s[z, e, s]
         mine = (name // faults) == me
-        first = jnp.where(mine, ons_s[z, s, e], jnp.int32(2**30))
+        first = jnp.where(mine, ons_s[z, e, s], jnp.int32(2**30))
         record = jnp.concatenate(
             [prior[z, s, pl.ds(e, 1), :], cur[z, s, pl.ds(e, 1), :]], axis=1
         )
@@ -188,7 +188,7 @@
         whole_wave(o).wait_recv()
     for o in range(1, sub_n):
         total = total + recv[o - 1]
-    out[...] = total
+    out[...] = jnp.swapaxes(total, 0, 1)
     for o in range(1, sub_n):
         whole_wave(o).wait_send()
         for c in same_tm(o):
@@ -212,15 +212,15 @@
         dma = pltpu.SemaphoreType.DMA
         waves = pl.pallas_call(
             functools.partial(synth_kernel, sub_n, tm_n),
-            out_shape=jax.ShapeDtypeStruct((scen_n, rows, span), jnp.float32),
+            out_shape=jax.ShapeDtypeStruct((rows, scen_n, span), jnp.float32),
             in_specs=[pl.BlockSpec(memory_space=pl.ANY)] * 4,
             out_specs=pl.BlockSpec(memory_space=pltpu.VMEM),
             scratch_shapes=[
                 pltpu.VMEM((faults, panel, taps), jnp.float32),
                 pltpu.VMEM((sub_n, scen_n, edev, span), jnp.float32),
                 pltpu.VMEM((sub_n, scen_n, edev, span), jnp.float32),
-                pltpu.SMEM((sub_n, scen_n, edev), jnp.int32),
-                pltpu.SMEM((sub_n, scen_n, edev), jnp.int32),
+                pltpu.SMEM((sub_n, edev, scen_n), jnp.int32),
+                pltpu.SMEM((sub_n, edev, scen_n), jnp.int32),
                 pltpu.VMEM((slots, taps // 2, span + taps // 2), jnp.bfloat16),
                 pltpu.VMEM((slots, taps // 2, span + taps // 2), jnp.bfloat16),
                 pltpu.VMEM((2 * panel, slots * taps), jnp.bfloat16),
@@ -230,8 +230,8 @@
                 dma((sub_n,)), dma((sub_n,)), dma((sub_n - 1,)), dma((sub_n - 1,)),
             ],
             compiler_params=pltpu.CompilerParams(collective_id=0, has_side_effects=True),
-        )(library, rates, subfault_ids, onsets)
-        return jnp.transpose(waves, (1, 0, 2))
+        )(library, rates, subfault_ids.T, onsets.T)
+        return waves
 
     in_specs = (
         P(("groups", "sub"), "gauge", None),

time: 30 us -> 26.8 us (0.89)
  local copies, waits for them, and re-layouts: 4.32 us -> 1.57 us
  Pallas kernels: 25.5 us -> 25.1 us
    transpose x1 -> x0, local copies, waits for them, and re-layouts: 1.64 us -> none  [on_device(): return jnp.transpose(waves, (1, 0, 2))]
    unnamed x2 -> x1, local copies, waits for them, and re-layouts: 2.68 us -> 1.57 us
    pallas_call x1, Pallas kernels: 25.5 us -> 25.1 us  [on_device(): pl.pallas_call(functools.partial(synth_kernel, sub_n, tm_n), out_shape=ja...]
where the time goes in v2:
time: 26.8 us; the launch traced here: 26.7 us
  Pallas kernels  25.1 us (94%)
  local copies, waits for them, and re-layouts  1.57 us (6%)
    pallas_call x1, Pallas kernels, on_device(): pl.pallas_call(functools.partial(synth_kernel, sub_n, tm_n), out_shape=ja...  25.1 us
    unnamed x1, local copies, waits for them, and re-layouts  1.57 us

profile of v2, /device:TPU:0, one launch (start us, length us, event | category | flops | bytes accessed | tf_op | source)
XLA Modules:
  0.0 26.7 jit_solution(8762555083860871474)
XLA Ops:
  0.0 25.1 %shard_map.46 = f32[16,8,256]{2,1,0:T(8,128)} custom-call(f32[128,64,256]{2,1,0:T(8,128)} %lib_hbm.1, f32[8,2,256]{2,1,0:T(2,128)} %rates.1, s32[2,8]{1,0:T(2,128)} %bitcast.2, s32[2,8]{1,0:T(2,128)} %bitcast.3), custom_call_target="tpu_custom_call" | custom-call | tf_op jit(solution)/shard_map/pallas_call | solution.py:213
  25.1 1.6 %copy.6 = f32[16,8,256]{2,1,0:T(8,128)} copy(f32[16,8,256]{2,1,0:T(8,128)} %shard_map.46) | data formatting | bytes 262144

commit v3 on v2

--- a/solution.py
+++ b/solution.py
@@ -12,8 +12,9 @@
 
 def synth_kernel(
     sub_n, tm_n, lib_hbm, rates, ids, onsets, out,
-    lib, cur, prior, ids_s, ons_s, toe_hi, toe_lo, green, part, recv,
-    lib_sem, own_sem, cur_send, cur_recv, prior_send, prior_recv, wave_send, wave_recv,
+    lib, cur, prior, ids_s, ons_s, toe_hi, toe_lo, green, skew, turns, part, direct, lent, joint, recv,
+    lib_sem, own_sem, cur_send, cur_recv, prior_send, prior_recv,
+    direct_sem, lend_send, lend_recv, wave_send, wave_recv,
 ):
     me = lax.axis_index("sub")
     core = lax.axis_index("tm")
@@ -21,6 +22,9 @@
     faults, panel, taps = lib.shape
     rows = panel // sub_n
     half = taps // 2
+    group = max(u for u in range(1, 5) if sub_n % u == 0)
+    slots = group * edev
+    rolled = half // 16 - turns.shape[0]
 
     lib_copy = pltpu.make_async_copy(lib_hbm, lib, lib_sem)
     lib_copy.start()
@@ -91,6 +95,13 @@
         for o in range(sub_n - 1, -1, -1):
             next_tm(o).start()
 
+    source = lax.broadcasted_iota(jnp.int32, (256, 128), 0)
+    target = lax.broadcasted_iota(jnp.int32, (256, 128), 1) + 128
+    for i in range(turns.shape[0]):
+        for h in range(2):
+            shift = 16 * (rolled + i) + 8 * h
+            turns[i, :, pl.ds(128 * h, 128)] = jnp.where(source == target - shift, 1.0, 0.0).astype(jnp.bfloat16)
+
     for c in own:
         c.wait()
     for o in range(1, sub_n):
@@ -117,7 +128,10 @@
         skewed = pltpu.roll(
             jnp.broadcast_to(record, (8, 2 * span)), 0, 1, stride=1, stride_axis=0
         )
-        for pair in range(half // 16):
+        top = skewed.astype(jnp.bfloat16).astype(jnp.float32)
+        skew[pl.ds(8 * slot, 8), :] = top
+        skew[pl.ds(8 * (slots + slot), 8), :] = skewed - top
+        for pair in range(rolled):
             two = [
                 (pltpu.roll(skewed, 16 * pair + 8 * h, 1) if pair + h else skewed)[:, half:]
                 for h in range(2)
@@ -134,8 +148,21 @@
             function - high.astype(jnp.float32)
         ).astype(jnp.bfloat16)
 
-    group = max(u for u in range(1, 5) if sub_n % u == 0)
-    slots = group * edev
+    def turned():
+        steps = half // 128 + span // 128
+        wide = jnp.concatenate(
+            [skew[:, pl.ds(128 * v, 256)] for v in range(steps)], axis=0
+        ).astype(jnp.bfloat16)
+        for pair in range(rolled, half // 16):
+            moved = jnp.dot(wide, turns[pair - rolled], preferred_element_type=jnp.float32)
+            for v in range(steps):
+                for h, toe in enumerate((toe_hi, toe_lo)):
+                    for slot in range(slots):
+                        row = 16 * slots * v + 8 * (slots * h + slot)
+                        piece = moved[row : row + 8]
+                        toe[slot, pl.ds(16 * pair, 16), pl.ds(128 * v, 128)] = jnp.concatenate(
+                            [piece[:, :128], piece[:, 128:]], axis=0
+                        ).astype(jnp.bfloat16)
 
     def stacked(toe):
         pieces = []
@@ -144,18 +171,54 @@
             pieces.append(toe[slot, :, pl.ds(0, span)])
         return jnp.concatenate(pieces, axis=0)
 
-    def wave_copy(s, o, dest, sent):
+    right = lax.rem(me, 2)
+    pair, pairs = me // 2, sub_n // 2
+    mate = me + 1 - 2 * right
+
+    def far_pair(o):
+        return lax.rem(pair + o, pairs)
+
+    def outer(o):
+        return jnp.where(far_pair(o) > pair, 1 - right, right) == 1
+
+    def remote(src, dst, send, recv_at, dest):
         return pltpu.make_async_remote_copy(
-            src_ref=part.at[s, dest],
-            dst_ref=recv.at[o - 1, s], send_sem=wave_send.at[o - 1], recv_sem=wave_recv.at[o - 1],
+            src_ref=src, dst_ref=dst, send_sem=send, recv_sem=recv_at,
             device_id={"sub": dest}, device_id_type=MESH,
         )
+
+    def to_mate(s):
+        return remote(part.at[s, mate], direct.at[s], direct_sem.at[0], direct_sem.at[1], mate)
+
+    def lend(s, o):
+        return remote(
+            part.at[s, pl.ds(2 * far_pair(o), 2)], lent.at[o - 1, s],
+            lend_send.at[o - 1], lend_recv.at[o - 1, s], mate,
+        )
+
+    def deliver(s, o, j):
+        return remote(
+            joint.at[o - 1, s, j], recv.at[o - 1, s],
+            wave_send.at[o - 1], wave_recv.at[o - 1], 2 * far_pair(o) + j,
+        )
+
+    def forward(s):
+        for o in range(1, pairs):
+            @pl.when(jnp.logical_not(outer(o)))
+            def _():
+                lend(s, o).wait_recv()
+                joint[o - 1, s] = part[s, pl.ds(2 * far_pair(o), 2)] + lent[o - 1, s]
+                deliver(s, o, 0).start()
+                deliver(s, o, 1).start()
+
+    lag = 2
 
     def scenario(s, carry):
         def block_group(first_z):
             for i in range(group):
                 for e in range(edev):
                     toeplitz(first_z + i, s, e, i * edev + e)
+            turned()
             big = jnp.dot(green[...], stacked(toe_hi), preferred_element_type=jnp.float32)
             small = jnp.dot(green[pl.ds(0, panel), :], stacked(toe_lo), preferred_element_type=jnp.float32)
             return big[:panel] + (big[panel:] + small)
@@ -171,26 +234,46 @@
                     part[s, d] += piece
                 return c
             lax.fori_loop(1, sub_n // group, more, 0)
-        for o in range(sub_n - 1, 0, -1):
-            wave_copy(s, o, peer(o), True).start()
+        for o in range(1, pairs):
+            @pl.when(outer(o))
+            def _():
+                lend(s, o).start()
+        to_mate(s).start()
+
+        @pl.when(s >= lag)
+        def _():
+            forward(s - lag)
         return carry
 
     lax.fori_loop(0, scen_n, scenario, 0)
 
-    def whole_wave(o):
-        return pltpu.make_async_remote_copy(
-            src_ref=recv.at[o - 1], dst_ref=recv.at[o - 1], send_sem=wave_send.at[o - 1],
-            recv_sem=wave_recv.at[o - 1], device_id={"sub": peer(o)}, device_id_type=MESH,
-        )
+    def rest(s, carry):
+        forward(s)
+        return carry
+
+    lax.fori_loop(scen_n - lag, scen_n, rest, 0)
+
+    def whole(ref, send, recv_at):
+        return remote(ref, ref, send, recv_at, mate)
 
     total = part[:, me]
-    for o in range(1, sub_n):
-        whole_wave(o).wait_recv()
-    for o in range(1, sub_n):
+    whole(direct, direct_sem.at[0], direct_sem.at[1]).wait_recv()
+    total = total + direct[...]
+    for o in range(1, pairs):
+        whole(recv.at[o - 1], wave_send.at[o - 1], wave_recv.at[o - 1]).wait_recv()
+    for o in range(1, pairs):
         total = total + recv[o - 1]
     out[...] = jnp.swapaxes(total, 0, 1)
+    whole(direct, direct_sem.at[0], direct_sem.at[1]).wait_send()
+    for o in range(1, pairs):
+        @pl.when(outer(o))
+        def _():
+            whole(lent.at[o - 1], lend_send.at[o - 1], wave_recv.at[o - 1]).wait_send()
+
+        @pl.when(jnp.logical_not(outer(o)))
+        def _():
+            whole(joint.at[o - 1], wave_send.at[o - 1], wave_recv.at[o - 1]).wait_send()
     for o in range(1, sub_n):
-        whole_wave(o).wait_send()
         for c in same_tm(o):
             c.wait_send()
 
@@ -208,12 +291,12 @@
         scen_n, edev, span = rates.shape
         rows = panel // sub_n
         group = max(u for u in range(1, 5) if sub_n % u == 0)
-        slots = group * edev
+        slots, pairs = group * edev, sub_n // 2
         dma = pltpu.SemaphoreType.DMA
         waves = pl.pallas_call(
             functools.partial(synth_kernel, sub_n, tm_n),
-            out_shape=jax.ShapeDtypeStruct((rows, scen_n, span), jnp.float32),
-            in_specs=[pl.BlockSpec(memory_space=pl.ANY)] * 4,
+            out_shape=pltpu.VMEM((rows, scen_n, span), jnp.float32),
+            in_specs=[pl.BlockSpec(memory_space=pltpu.HBM)] * 4,
             out_specs=pl.BlockSpec(memory_space=pltpu.VMEM),
             scratch_shapes=[
                 pltpu.VMEM((faults, panel, taps), jnp.float32),
@@ -224,13 +307,19 @@
                 pltpu.VMEM((slots, taps // 2, span + taps // 2), jnp.bfloat16),
                 pltpu.VMEM((slots, taps // 2, span + taps // 2), jnp.bfloat16),
                 pltpu.VMEM((2 * panel, slots * taps), jnp.bfloat16),
+                pltpu.VMEM((16 * slots, 2 * span), jnp.float32),
+                pltpu.VMEM((taps // 32 - taps * 6 // 256, 256, 256), jnp.bfloat16),
                 pltpu.VMEM((scen_n, sub_n, rows, span), jnp.float32),
-                pltpu.VMEM((sub_n - 1, scen_n, rows, span), jnp.float32),
+                pltpu.VMEM((scen_n, rows, span), jnp.float32),
+                pltpu.VMEM((pairs - 1, scen_n, 2, rows, span), jnp.float32),
+                pltpu.VMEM((pairs - 1, scen_n, 2, rows, span), jnp.float32),
+                pltpu.VMEM((pairs - 1, scen_n, rows, span), jnp.float32),
                 dma, dma((3,)), dma((3, sub_n - 1)), dma((3, sub_n - 1)),
-                dma((sub_n,)), dma((sub_n,)), dma((sub_n - 1,)), dma((sub_n - 1,)),
+                dma((sub_n,)), dma((sub_n,)), dma((2,)), dma((pairs - 1,)), dma((pairs - 1, scen_n)),
+                dma((pairs - 1,)), dma((pairs - 1,)),
             ],
-            compiler_params=pltpu.CompilerParams(collective_id=0, has_side_effects=True),
-        )(library, rates, subfault_ids.T, onsets.T)
+            compiler_params=pltpu.CompilerParams(collective_id=0, has_side_effects=True, vmem_limit_bytes=40 * 2**20),
+        )(*(pltpu.with_memory_space_constraint(x, pltpu.HBM) for x in (library, rates, subfault_ids.T, onsets.T)))
         return waves
 
     in_specs = (

time: 26.8 us -> 25 us (0.933)
  local copies, waits for them, and re-layouts: 1.57 us -> 0.66 us
  Pallas kernels: 25.1 us -> 24.2 us
    pallas_call x1, Pallas kernels: 25.1 us -> 24.2 us  [on_device(): pl.pallas_call(functools.partial(synth_kernel, sub_n, tm_n), out_shape=pl...]
    unnamed x1, local copies, waits for them, and re-layouts: 1.57 us -> 0.66 us
where the time goes in v3:
time: 25 us; the launch traced here: 24.8 us
  Pallas kernels  24.2 us (97%)
  local copies, waits for them, and re-layouts  0.66 us (3%)
    pallas_call x1, Pallas kernels, on_device(): pl.pallas_call(functools.partial(synth_kernel, sub_n, tm_n), out_shape=pl...  24.2 us
    unnamed x1, local copies, waits for them, and re-layouts  0.66 us

profile of v3, /device:TPU:0, one launch (start us, length us, event | category | flops | bytes accessed | tf_op | source)
XLA Modules:
  0.0 24.8 jit_solution(16819399522733048699)
XLA Ops:
  0.0 24.2 %shard_map.46 = f32[16,8,256]{2,1,0:T(8,128)S(1)} custom-call(f32[128,64,256]{2,1,0:T(8,128)} %lib_hbm.1, f32[8,2,256]{2,1,0:T(2,128)} %rates.1, s32[2,8]{1,0:T(2,128)} %bitcast.2, s32[2,8]{1,0:T(2,128)} %bitcast.3), custom_call_target="tpu_custom_call" | custom-call | tf_op jit(solution)/shard_map/pallas_call | solution.py:296
  24.2 0.7 %copy.6 = f32[16,8,256]{2,1,0:T(8,128)} copy(f32[16,8,256]{2,1,0:T(8,128)S(1)} %shard_map.46) | data formatting | bytes 262144

commit v4 on v3

--- a/solution.py
+++ b/solution.py
@@ -26,6 +26,20 @@
     slots = group * edev
     rolled = half // 16 - turns.shape[0]
 
+    barrier = pltpu.get_barrier_semaphore()
+
+    def peer(o):
+        return lax.rem(me + o, sub_n)
+
+    for o in range(1, sub_n):
+        pl.semaphore_signal(barrier, inc=1, device_id={"sub": peer(o)}, device_id_type=MESH)
+    for step in (-1, 1):
+        @pl.when((core + step >= 0) & (core + step < tm_n))
+        def _():
+            for o in range(sub_n):
+                pl.semaphore_signal(
+                    barrier, inc=1, device_id={"sub": peer(o), "tm": core + step}, device_id_type=MESH
+                )
     lib_copy = pltpu.make_async_copy(lib_hbm, lib, lib_sem)
     lib_copy.start()
     own = [
@@ -35,22 +49,11 @@
     ]
     for c in own:
         c.start()
-    prior[...] = jnp.zeros_like(prior)
-
-    barrier = pltpu.get_barrier_semaphore()
-
-    def peer(o):
-        return lax.rem(me + o, sub_n)
-
-    for o in range(1, sub_n):
-        pl.semaphore_signal(barrier, inc=1, device_id={"sub": peer(o)}, device_id_type=MESH)
-    for step in (-1, 1):
-        @pl.when((core + step >= 0) & (core + step < tm_n))
-        def _():
-            for o in range(sub_n):
-                pl.semaphore_signal(
-                    barrier, inc=1, device_id={"sub": peer(o), "tm": core + step}, device_id_type=MESH
-                )
+
+    @pl.when(core == 0)
+    def _():
+        prior[...] = jnp.zeros_like(prior)
+
     ends = jnp.where(core > 0, sub_n, 0) + jnp.where(core < tm_n - 1, sub_n, 0)
     pl.semaphore_wait(barrier, sub_n - 1 + ends)
 
@@ -211,7 +214,7 @@
                 deliver(s, o, 0).start()
                 deliver(s, o, 1).start()
 
-    lag = 2
+    lag = 1
 
     def scenario(s, carry):
         def block_group(first_z):

time: 25 us -> 24.9 us (level)
  no operation moved by 1% of the time
where the time goes in v4:
time: 24.9 us; the launch traced here: 24.8 us
  Pallas kernels  24.1 us (97%)
  local copies, waits for them, and re-layouts  0.66 us (3%)
    pallas_call x1, Pallas kernels, on_device(): pl.pallas_call(functools.partial(synth_kernel, sub_n, tm_n), out_shape=pl...  24.1 us
    unnamed x1, local copies, waits for them, and re-layouts  0.66 us

profile of v4, /device:TPU:0, one launch (start us, length us, event | category | flops | bytes accessed | tf_op | source)
XLA Modules:
  0.0 24.8 jit_solution(601212698848056317)
XLA Ops:
  0.0 24.1 %shard_map.46 = f32[16,8,256]{2,1,0:T(8,128)S(1)} custom-call(f32[128,64,256]{2,1,0:T(8,128)} %lib_hbm.1, f32[8,2,256]{2,1,0:T(2,128)} %rates.1, s32[2,8]{1,0:T(2,128)} %bitcast.2, s32[2,8]{1,0:T(2,128)} %bitcast.3), custom_call_target="tpu_custom_call" | custom-call | tf_op jit(solution)/shard_map/pallas_call | solution.py:299
  24.1 0.7 %copy.6 = f32[16,8,256]{2,1,0:T(8,128)} copy(f32[16,8,256]{2,1,0:T(8,128)S(1)} %shard_map.46) | data formatting | bytes 262144
